TPU v7x, 32 devices: a whole 2x2x4 slice. The times are simulated.
32 devices in a mesh: fsdp: 8 (over y, x, core), ulysses: 4 (over z).
Axes of the slice: x: 2, y: 2, z: 4, core: 2. Of those that a mesh axis runs over, the one named last changes fastest.
Arguments:
- layer_input: bfloat16 [24, 1024, 2048], P('fsdp', 'ulysses'), may hold values from -6 to 6
- cotangent: bfloat16 [24, 1024, 2048], P('fsdp', 'ulysses'), may hold values from -6 to 6
- positions: int32 [24, 1024], P('fsdp', 'ulysses'), may hold values from 0 to 4095
- block_ids: int32 [24, 1024], P('fsdp'), may hold values from 0 to 7, never falling along the last dimension, each value on 1 to 256 neighbouring positions
- skip_mask: int32 [24], P('fsdp'), may hold values 0 or 1
- attn_gain: bfloat16 [2048], P('fsdp'), may hold values from 0.5 to 1.5
- w_query: bfloat16 [2048, 2048], P('fsdp'), may hold values from -0.125 to 0.125
- w_key: bfloat16 [2048, 512], P('fsdp'), may hold values from -0.125 to 0.125
- w_value: bfloat16 [2048, 512], P('fsdp'), may hold values from -0.125 to 0.125
- w_out: bfloat16 [2048, 2048], P('fsdp'), may hold values from -1 to 1
- mlp_gain: bfloat16 [2048], P('fsdp'), may hold values from 0.5 to 1.5
- w_gate: bfloat16 [2048, 5632], P('fsdp'), may hold values from -0.125 to 0.125
- w_up: bfloat16 [2048, 5632], P('fsdp'), may hold values from -0.125 to 0.125
- w_down: bfloat16 [5632, 2048], P(None, 'fsdp'), may hold values from -0.078125 to 0.078125
Outputs:
- output: bfloat16 [24, 1024, 2048], P('fsdp', 'ulysses')
- grad_input: bfloat16 [24, 1024, 2048], P('fsdp', 'ulysses')
- grad_attn_gain: float32 [2048], P('fsdp')
- grad_w_query: float32 [2048, 2048], P('fsdp')
- grad_w_key: float32 [2048, 512], P('fsdp')
- grad_w_value: float32 [2048, 512], P('fsdp')
- grad_w_out: float32 [2048, 2048], P('fsdp')
- grad_mlp_gain: float32 [2048], P('fsdp')
- grad_w_gate: float32 [2048, 5632], P('fsdp')
- grad_w_up: float32 [2048, 5632], P('fsdp')
- grad_w_down: float32 [5632, 2048], P(None, 'fsdp')
Inputs may be any that keep to these rules, and one draw needn't show every extreme that they name: `block_ids`: within a sequence block numbers never fall, every number of 0 to 7 occurs, and a block has 1 to 256 tokens.
All inputs are finite; a program needn't handle non-finite values. No bound on the sum of `skip_mask` on one device may be relied on, other than what follows from the above.
Results may differ from a plain program's by a relative error of at most 0.022.
Values may be sent and summed in bfloat16 or wider, within the bound.
No kernel may reach another device: no remote copies, remote signals or barrier semaphores. Data moves between devices by JAX's collectives and lax.ppermute only.
A program may use at most 640 MiB of HBM per device.

v0:
```python
import math
import jax
import jax.numpy as jnp
from jax import lax
from jax.sharding import PartitionSpec as P

H = 16
KVH = 4
HD = 128
epsilon = 1e-05


def rotary_tables(token_positions, head_size):
    half_size = head_size // 2
    frequency = jnp.exp(
        jnp.arange(half_size, dtype=jnp.float32) * (-2.0 * math.log(10000.0) / head_size)
    )
    angles = token_positions.astype(jnp.float32)[..., None] * frequency
    cosine = jnp.concatenate([jnp.cos(angles), jnp.cos(angles)], -1)
    sine_table = jnp.concatenate([jnp.sin(angles), jnp.sin(angles)], -1)
    return (cosine, sine_table)


def rotate(values, cosine, sine_table):
    half_size = values.shape[-1] // 2
    turned = jnp.concatenate([-values[..., half_size:], values[..., :half_size]], -1)
    return values * cosine[..., None, :] + turned * sine_table[..., None, :]


def unrotate(gradients, cosine, sine_table):
    half_size = gradients.shape[-1] // 2
    scaled = gradients * sine_table[..., None, :]
    turned = jnp.concatenate([scaled[..., half_size:], -scaled[..., :half_size]], -1)
    return gradients * cosine[..., None, :] + turned


def on_device(
    layer_input,
    cotangent,
    positions,
    block_ids,
    skip_mask,
    attn_gain,
    w_query,
    w_key,
    w_value,
    w_out,
    mlp_gain,
    w_gate,
    w_up,
    w_down,
):
    seq_count, local_len, width = layer_input.shape
    row_total = seq_count * local_len
    fsdp_size = lax.axis_size("fsdp")
    ulysses_size = lax.axis_size("ulysses")
    repeat_count = max(1, ulysses_size // KVH)
    head_scale = 1.0 / math.sqrt(HD)
    query_width = H * HD
    pair_width = KVH * HD
    hidden_width = w_gate.shape[1]
    gain_one, query_full, key_full, value_full, out_full = (
        lax.all_gather(attn_gain, "fsdp", axis=0, tiled=True),
        lax.all_gather(w_query, "fsdp", axis=0, tiled=True),
        lax.all_gather(w_key, "fsdp", axis=0, tiled=True),
        lax.all_gather(w_value, "fsdp", axis=0, tiled=True),
        lax.all_gather(w_out, "fsdp", axis=0, tiled=True),
    )
    keep_rows = jnp.repeat((1 - skip_mask).astype(jnp.float32), local_len)[:, None]
    inputs_flat = layer_input.astype(jnp.float32).reshape(row_total, width)
    inv_one = lax.rsqrt(jnp.mean(inputs_flat * inputs_flat, -1, keepdims=True) + epsilon)
    unit_one = inputs_flat * inv_one
    normed_one = (unit_one * gain_one.astype(jnp.float32)).astype(jnp.bfloat16)
    query_pre = jnp.dot(normed_one, query_full, preferred_element_type=jnp.float32).reshape(
        seq_count, local_len, H, HD
    )
    key_pre = jnp.dot(normed_one, key_full, preferred_element_type=jnp.float32).reshape(
        seq_count, local_len, KVH, HD
    )
    value_pre = jnp.dot(normed_one, value_full, preferred_element_type=jnp.float32).reshape(
        seq_count, local_len, KVH, HD
    )
    cosine, sine_table = rotary_tables(positions, HD)
    query_sent = rotate(query_pre, cosine, sine_table).astype(jnp.bfloat16)
    key_sent = jnp.repeat(rotate(key_pre, cosine, sine_table), repeat_count, axis=2).astype(
        jnp.bfloat16
    )
    value_sent = jnp.repeat(value_pre, repeat_count, axis=2).astype(jnp.bfloat16)
    query_heads, key_heads, value_heads = (
        lax.all_to_all(query_sent, "ulysses", split_axis=2, concat_axis=1, tiled=True),
        lax.all_to_all(key_sent, "ulysses", split_axis=2, concat_axis=1, tiled=True),
        lax.all_to_all(value_sent, "ulysses", split_axis=2, concat_axis=1, tiled=True),
    )
    full_len = query_heads.shape[1]
    local_heads = query_heads.shape[2]
    local_slots = key_heads.shape[2]
    group_size = local_heads // local_slots

    def scores_for(query_seq, key_seq, block_row):
        grouped = query_seq.reshape(full_len, local_slots, group_size, HD)
        raw_scores = (
            jnp.einsum("qsgd,ksd->sgqk", grouped, key_seq, preferred_element_type=jnp.float32)
            * head_scale
        )
        allowed = block_row[None, :] <= block_row[:, None]
        return jnp.where(allowed, raw_scores, -1e30)

    def attend(record):
        query_seq, key_seq, value_seq, block_row = record
        scores = scores_for(query_seq, key_seq, block_row)
        largest = jnp.max(scores, -1, keepdims=True)
        exponent = jnp.exp(scores - largest)
        row_sums = jnp.sum(exponent, -1, keepdims=True)
        chances = (exponent / row_sums).astype(jnp.bfloat16)
        mixture = jnp.einsum(
            "sgqk,ksd->qsgd", chances, value_seq, preferred_element_type=jnp.float32
        )
        log_total = (largest + jnp.log(row_sums))[..., 0]
        return (mixture.reshape(full_len, local_heads, HD).astype(jnp.bfloat16), log_total)

    attn_heads, log_totals = lax.map(attend, (query_heads, key_heads, value_heads, block_ids))
    attended_tokens = lax.all_to_all(attn_heads, "ulysses", split_axis=1, concat_axis=2, tiled=True)
    attended = attended_tokens.reshape(row_total, query_width)
    branch_attn = jnp.dot(attended, out_full, preferred_element_type=jnp.float32)
    middle = inputs_flat + keep_rows * branch_attn
    inv_two = lax.rsqrt(jnp.mean(middle * middle, -1, keepdims=True) + epsilon)
    unit_two = middle * inv_two
    gain_piece = lax.all_gather(mlp_gain, "fsdp", axis=0, tiled=True)
    gate_piece = lax.all_gather(w_gate, "fsdp", axis=0, tiled=True)
    up_piece = lax.all_gather(w_up, "fsdp", axis=0, tiled=True)
    gain_float = gain_piece.astype(jnp.float32)
    normed_piece = (unit_two * gain_float).astype(jnp.bfloat16)
    gate_sum = jnp.dot(normed_piece, gate_piece, preferred_element_type=jnp.float32)
    up_sum = jnp.dot(normed_piece, up_piece, preferred_element_type=jnp.float32)
    sigmoid_gate = jax.nn.sigmoid(gate_sum)
    silu_gate = gate_sum * sigmoid_gate
    hidden = (silu_gate * up_sum).astype(jnp.bfloat16)
    branch_mlp = jnp.dot(
        hidden,
        lax.all_gather(w_down, "fsdp", axis=1, tiled=True),
        preferred_element_type=jnp.float32,
    )
    output = (middle + keep_rows * branch_mlp).astype(jnp.bfloat16).reshape(layer_input.shape)
    grad_out = cotangent.astype(jnp.float32).reshape(row_total, width)
    grad_mlp = (keep_rows * grad_out).astype(jnp.bfloat16)
    grad_hidden = jnp.einsum(
        "rc,fc->rf",
        grad_mlp,
        lax.all_gather(w_down, "fsdp", axis=1, tiled=True),
        preferred_element_type=jnp.float32,
    )
    grad_gate = (
        grad_hidden * up_sum * sigmoid_gate * (1.0 + gate_sum * (1.0 - sigmoid_gate))
    ).astype(jnp.bfloat16)
    grad_up = (grad_hidden * silu_gate).astype(jnp.bfloat16)
    stacked_in = jnp.stack([w_gate, w_up])
    shard_piece = lax.all_gather(stacked_in, "fsdp", axis=1, tiled=True)
    from_gate = jnp.einsum(
        "rf,cf->rc", grad_gate, shard_piece[0], preferred_element_type=jnp.float32
    )
    grad_normed_two = from_gate + jnp.einsum(
        "rf,cf->rc", grad_up, shard_piece[1], preferred_element_type=jnp.float32
    )
    grad_unit_two = grad_normed_two * gain_float
    grad_gain_two = jnp.sum(grad_normed_two * unit_two, 0)
    grad_middle = grad_out + inv_two * (
        grad_unit_two - unit_two * jnp.mean(grad_unit_two * unit_two, -1, keepdims=True)
    )
    grad_branch = (keep_rows * grad_middle).astype(jnp.bfloat16)
    grad_attended = jnp.einsum(
        "rd,cd->rc", grad_branch, out_full, preferred_element_type=jnp.float32
    )
    grad_attended = grad_attended.astype(jnp.bfloat16).reshape(seq_count, local_len, H, HD)
    grad_heads = lax.all_to_all(grad_attended, "ulysses", split_axis=2, concat_axis=1, tiled=True)

    def attend_back(record):
        query_seq, key_seq, value_seq, block_row, log_total, grad_seq = record
        scores = scores_for(query_seq, key_seq, block_row)
        chances = jnp.exp(scores - log_total[..., None])
        grouped = query_seq.reshape(full_len, local_slots, group_size, HD)
        grouped_grad = grad_seq.reshape(full_len, local_slots, group_size, HD)
        grad_chances = jnp.einsum(
            "qsgd,ksd->sgqk", grouped_grad, value_seq, preferred_element_type=jnp.float32
        )
        center = jnp.sum(chances * grad_chances, -1, keepdims=True)
        grad_scores = (chances * (grad_chances - center)).astype(jnp.bfloat16)
        grad_query = (
            jnp.einsum("sgqk,ksd->qsgd", grad_scores, key_seq, preferred_element_type=jnp.float32)
            * head_scale
        )
        grad_key = (
            jnp.einsum("sgqk,qsgd->ksd", grad_scores, grouped, preferred_element_type=jnp.float32)
            * head_scale
        )
        grad_value = jnp.einsum(
            "sgqk,qsgd->ksd",
            chances.astype(jnp.bfloat16),
            grouped_grad,
            preferred_element_type=jnp.float32,
        )
        return (
            grad_query.reshape(full_len, local_heads, HD).astype(jnp.bfloat16),
            grad_key.astype(jnp.bfloat16),
            grad_value.astype(jnp.bfloat16),
        )

    grad_query_heads, grad_key_heads, grad_value_heads = lax.map(
        attend_back, (query_heads, key_heads, value_heads, block_ids, log_totals, grad_heads)
    )
    grad_query_tok, grad_key_tok, grad_value_tok = (
        lax.all_to_all(grad_query_heads, "ulysses", split_axis=1, concat_axis=2, tiled=True),
        lax.all_to_all(grad_key_heads, "ulysses", split_axis=1, concat_axis=2, tiled=True),
        lax.all_to_all(grad_value_heads, "ulysses", split_axis=1, concat_axis=2, tiled=True),
    )
    grad_key_sum = (
        grad_key_tok.astype(jnp.float32).reshape(seq_count, local_len, KVH, repeat_count, HD).sum(3)
    )
    grad_value_sum = (
        grad_value_tok.astype(jnp.float32)
        .reshape(seq_count, local_len, KVH, repeat_count, HD)
        .sum(3)
    )
    grad_query_pre = (
        unrotate(grad_query_tok.astype(jnp.float32), cosine, sine_table)
        .astype(jnp.bfloat16)
        .reshape(row_total, query_width)
    )
    grad_key_pre = (
        unrotate(grad_key_sum, cosine, sine_table)
        .astype(jnp.bfloat16)
        .reshape(row_total, pair_width)
    )
    grad_value_pre = grad_value_sum.astype(jnp.bfloat16).reshape(row_total, pair_width)
    grad_normed_one = jnp.einsum(
        "rc,dc->rd", grad_query_pre, query_full, preferred_element_type=jnp.float32
    )
    grad_normed_one = grad_normed_one + jnp.einsum(
        "rc,dc->rd", grad_key_pre, key_full, preferred_element_type=jnp.float32
    )
    grad_normed_one = grad_normed_one + jnp.einsum(
        "rc,dc->rd", grad_value_pre, value_full, preferred_element_type=jnp.float32
    )
    grad_unit_one = grad_normed_one * gain_one.astype(jnp.float32)
    grad_gain_one = jnp.sum(grad_normed_one * unit_one, 0)
    grad_input = grad_middle + inv_one * (
        grad_unit_one - unit_one * jnp.mean(grad_unit_one * unit_one, -1, keepdims=True)
    )
    grad_input = grad_input.astype(jnp.bfloat16).reshape(layer_input.shape)
    gain_totals = lax.psum(jnp.stack([grad_gain_one, grad_gain_two]), ("fsdp", "ulysses"))
    owner_rows = width // fsdp_size
    gain_shard = lax.dynamic_slice_in_dim(
        gain_totals, lax.axis_index("fsdp") * owner_rows, owner_rows, 1
    )
    grad_attn_mid = jnp.concatenate([grad_query_pre, grad_key_pre, grad_value_pre], 1)
    grad_mlp_mid = jnp.concatenate([grad_gate, grad_up], 1)
    owner_sums = lax.psum_scatter(
        jnp.concatenate(
            [
                jnp.einsum(
                    "rc,re->ce", normed_one, grad_attn_mid, preferred_element_type=jnp.float32
                ),
                jnp.einsum("rc,re->ce", attended, grad_branch, preferred_element_type=jnp.float32),
                jnp.einsum(
                    "rc,re->ce", normed_piece, grad_mlp_mid, preferred_element_type=jnp.float32
                ),
                jnp.einsum("rc,re->ce", grad_mlp, hidden, preferred_element_type=jnp.float32),
            ],
            1,
        ).astype(jnp.bfloat16),
        "fsdp",
        scatter_dimension=0,
        tiled=True,
    ).astype(jnp.float32)
    owner_sums = lax.psum(owner_sums.astype(jnp.bfloat16), "ulysses").astype(jnp.float32)
    first_value = query_width + pair_width
    first_out = first_value + pair_width
    first_gate = first_out + width
    first_up = first_gate + hidden_width
    first_down = first_up + hidden_width
    return (
        output,
        grad_input,
        gain_shard[0],
        owner_sums[:, :query_width],
        owner_sums[:, query_width:first_value],
        owner_sums[:, first_value:first_out],
        owner_sums[:, first_out:first_gate],
        gain_shard[1],
        owner_sums[:, first_gate:first_up],
        owner_sums[:, first_up:first_down],
        owner_sums[:, first_down : first_down + hidden_width].T,
    )


def solution(mesh):
    return jax.shard_map(
        on_device,
        mesh=mesh,
        in_specs=(
            P("fsdp", "ulysses", None),
            P("fsdp", "ulysses", None),
            P("fsdp", "ulysses"),
            P("fsdp", None),
            P("fsdp"),
            P("fsdp"),
            P("fsdp", None),
            P("fsdp", None),
            P("fsdp", None),
            P("fsdp", None),
            P("fsdp"),
            P("fsdp", None),
            P("fsdp", None),
            P(None, "fsdp"),
        ),
        out_specs=(
            P("fsdp", "ulysses", None),
            P("fsdp", "ulysses", None),
            P("fsdp"),
            P("fsdp", None),
            P("fsdp", None),
            P("fsdp", None),
            P("fsdp", None),
            P("fsdp"),
            P("fsdp", None),
            P("fsdp", None),
            P(None, "fsdp"),
        ),
        check_vma=False,
    )
```

profile of v0, /device:TPU:0, one launch (start us, length us, event | category | flops | bytes accessed | tf_op | source)
XLA Modules:
  0.0 2315.7 jit_solution(7480973175895499666)
XLA Ops:
  55.5 14.9 all-gather.13.cloned.1.call-done
  79.3 47.4 %all-gather.15.cloned.1.call-done = bf16[2048,2048]{1,0:T(8,128)(2,1)} async-done(((bf16[256,2048]{1,0:T(8,128)(2,1)}), bf16[2048,2048]{1,0:T(8,128)(2,1)}) %all-gather.15.cloned.1.call-update) | async-done | bytes 8388624 | tf_op jit(solution)/shard_map/all_gather | solution.py:64
  126.7 12.4 copy.162
  172.7 66.7 %all-to-all-done.2 = bf16[3,256,16,128]{1,3,0,2:T(8,128)(2,1)} async-done(((bf16[3,256,16,128]{1,3,0,2:T(8,128)(2,1)}), bf16[3,256,16,128]{1,3,0,2:T(8,128)(2,1)}, u32[]{:S(2)}, u32[]{:S(2)}) %all-to-all-start.2) | async-done | bytes 3145760 | tf_op jit(solution)/shard_map/all_to_all | solution.py:90
  246.5 55.1 %while.26 = (s32[]{:T(128)}, bf16[3,1024,4,128]{3,2,0,1:T(4,128)(2,1)}, f32[3,1,4,1024]{3,2,1,0:T(4,128)}, bf16[3,1024,1,128]{3,1,0,2:T(8,128)(2,1)}, s32[3,1024...) while((s32[]{:T(128)}, ...), condition=%wide.region_4.5_spmd, body=%wide.region_1.4_spmd.sunk | while | flops 2199384064 | bytes 61486188 | solution.py:121
  319.6 57.0 %all-to-all-done.3 = bf16[3,1024,4,128]{3,2,0,1:T(4,128)(2,1)} async-done(((bf16[3,1024,4,128]{3,2,0,1:T(4,128)(2,1)}), bf16[3,1024,4,128]{3,2,0,1:T(4,128)(2,1)}, u32[]{:S(2)}, u32[]{:S(2)}) %all-to-all-start.3) | async-done | bytes 3145760 | tf_op jit(solution)/shard_map/all_to_all | solution.py:122
  387.7 10.5 multiply_reduce_fusion.2
  401.5 26.0 %fusion.115 = f32[768,5632]{1,0:T(8,128)} fusion(bf16[768,2048]{1,0:T(8,128)(2,1)S(1)} %multiply_convert_fusion.5, bf16[2048,5632]{1,0:T(8,128)(2,1)} %all-gather.21.cloned.1.call-done), kind=kOutput, calls=%fused_computation.174 | convolution fusion | flops 17716740096 | bytes 43515904 | tf_op jit(solution)/shard_map/dot_general | solution.py:134
  427.6 25.9 %fusion.116 = f32[768,5632]{1,0:T(8,128)} fusion(bf16[768,2048]{1,0:T(8,128)(2,1)} %fusion.73, bf16[5632,2048]{1,0:T(8,128)(2,1)} %all-gather.23.cloned.1.call-done), kind=kOutput, calls=%fused_computation.175 | convolution fusion | flops 17716740096 | bytes 43515904 | tf_op jit(solution)/shard_map/rc,fc->rf/dot_general | solution.py:146
  453.5 88.7 %all-gather.19.cloned.1.call-done = bf16[2048,5632]{1,0:T(8,128)(2,1)} async-done(((bf16[256,5632]{1,0:T(8,128)(2,1)}), bf16[2048,5632]{1,0:T(8,128)(2,1)}) %all-gather.19.cloned.1.call-update) | async-done | bytes 23068688 | tf_op jit(solution)/shard_map/all_gather | solution.py:129
  542.2 40.9 %multiply_convert_fusion.2 = (bf16[768,5632]{1,0:T(8,128)(2,1)}, bf16[768,5632]{1,0:T(8,128)(2,1)}, bf16[768,5632]{1,0:T(8,128)(2,1)}) fusion(f32[768,5632]{1,0:T(8,128)} %fusion.116, f32[768,5632]{1,0:T(8,128)} %fusion.115, bf16[768,2048]{1,0:T(8,128)(2,1)S(1)} %multiply_convert_fusion.5, bf16[2048,5632]{1,0:T(8,128)(2,1)} %all-gather.19.cloned.1.call-done), kind=kOutput, calls=%fused_computation.82 | convolution fusion | flops 17781620736 | bytes 86769664 | tf_op jit(solution)/shard_map/dot_general | solution.py:133
  583.1 175.8 %all-gather.25.cloned.1.call-done = bf16[2,2048,5632]{2,1,0:T(8,128)(2,1)} async-done(((bf16[2,256,5632]{2,1,0:T(8,128)(2,1)}), bf16[2,2048,5632]{2,1,0:T(8,128)(2,1)}) %all-gather.25.cloned.1.call-update) | async-done | bytes 46137360 | tf_op jit(solution)/shard_map/all_gather | solution.py:157
  758.8 25.1 %fusion.67 = f32[768,2048]{1,0:T(8,128)} fusion(bf16[768,5632]{1,0:T(8,128)(2,1)} %get-tuple-element.291, bf16[2,2048,5632]{2,1,0:T(8,128)(2,1)} %all-gather.25.cloned.1.call-done), kind=kOutput, calls=%fused_computation.74 | convolution fusion | flops 17716740096 | bytes 38010880 | tf_op jit(solution)/shard_map/rf,cf->rc/dot_general | solution.py:161
  784.0 27.1 %multiply_reduce_fusion = (f32[2048]{0:T(1024)}, f32[768]{0:T(1024)S(1)}, f32[768,2048]{1,0:T(8,128)}) fusion(f32[768,2048]{1,0:T(8,128)S(1)} %copy-done.8, f32[768]{0:T(1024)S(1)} %copy-done.31, f32[2048]{0:T(1024)S(1)} %bitcast.438, f32[768,2048]{1,0:T(8,128)} %fusion.67, bf16[768,5632]{1,0:T(8,128)(2,1)} %get-tuple-element.290, ...), kind=kOutput, calls=%fused_computation.117 | convolution fusion | flops 17727748096 | bytes 50616320 | tf_op jit(solution)/shard_map/rf,cf->rc/dot_general | solution.py:158
  815.7 11.4 fusion.98
  835.2 71.1 %all-to-all-done.4 = bf16[3,256,16,128]{3,1,0,2:T(8,128)(2,1)S(1)} async-done(((bf16[3,256,16,128]{3,1,0,2:T(8,128)(2,1)}), bf16[3,256,16,128]{3,1,0,2:T(8,128)(2,1)S(1)}, u32[]{:S(2)}, u32[]{:S(2)}) %all-to-all-start.4) | async-done | bytes 3145760 | tf_op jit(solution)/shard_map/all_to_all | solution.py:174
  912.5 179.5 %while.27 = (s32[]{:T(128)}, bf16[3,1024,4,128]{3,2,0,1:T(4,128)(2,1)}, bf16[3,1024,1,128]{1,3,2,0:T(8,128)(2,1)}, bf16[3,1024,1,128]{1,3,2,0:T(8,128)(2,1)}, bf...) while((s32[]{:T(128)}, ...), condition=%wide.region_9.10_spmd, body=%wide.region_7.9_spmd.sunk | while | flops 5408944128 | bytes 264601872 | solution.py:207
  934.3 13.6 fusion.185
  994.0 13.6 fusion.185
  1053.7 13.6 fusion.185
  1102.7 20.5 all-to-all-done.7
  1126.7 44.9 %convolution_convert_fusion = bf16[2048,11264]{1,0:T(8,128)(2,1)} fusion(bf16[768,2048]{1,0:T(8,128)(2,1)} %copy-done.22, bf16[768,5632]{1,0:T(8,128)(2,1)} %get-tuple-element.291, bf16[768,5632]{1,0:T(8,128)(2,1)} %get-tuple-element.290), kind=kOutput, calls=%fused_computation.72 | convolution fusion | flops 35491151872 | bytes 66584576 | tf_op jit(solution)/shard_map/rc,re->ce/dot_general | solution.py:263
  1177.6 26.4 %convolution_convert_fusion.1 = bf16[2048,5632]{1,0:T(8,128)(2,1)} fusion(bf16[768,2048]{1,0:T(8,128)(2,1)} %fusion.73, bf16[768,5632]{1,0:T(8,128)(2,1)} %get-tuple-element.292), kind=kOutput, calls=%fused_computation.77 | convolution fusion | flops 17728274432 | bytes 34865152 | tf_op jit(solution)/shard_map/rc,re->ce/dot_general | solution.py:266
  1204.0 12.2 convolution_convert_fusion.3
  1216.2 12.3 copy.187
  1305.7 10.9 fusion.117
  1327.1 13.4 convolution_convert_fusion.2
  1340.5 59.2 %pad_maximum_fusion = bf16[2048,22016]{1,0:T(8,128)(2,1)} fusion(bf16[2048,5632]{1,0:T(8,128)(2,1)} %convolution_convert_fusion.1, bf16[2048,11264]{1,0:T(8,128)(2,1)} %convolution_convert_fusion, bf16[2048,2048]{1,0:T(8,128)(2,1)} %copy.187, bf16[2048,3072]{1,0:T(8,128)(2,1)} %convolution_convert_fusion.2), kind=kLoop, calls=%fused_computation.71 | loop fusion | flops 360710144 | bytes 180355072 | tf_op jit(solution)/shard_map/concatenate | solution.py:257
  1399.8 490.7 %reduce-scatter.4.cloned.1.call-done = bf16[256,22016]{1,0:T(8,128)(2,1)} async-done(((bf16[2048,22016]{1,0:T(8,128)(2,1)}), bf16[256,22016]{1,0:T(8,128)(2,1)}) %reduce-scatter.4.cloned.1.call-update) | async-done | bytes 11272208
  1890.6 25.1 %add_convert_fusion = bf16[768,2048]{1,0:T(8,128)(2,1)} fusion(f32[768,2048]{1,0:T(8,128)} %copy-done.7, bf16[768,5632]{1,0:T(8,128)(2,1)} %get-tuple-element.292, bf16[5632,2048]{1,0:T(8,128)(2,1)} %all-gather.23.cloned.1.call-done, f32[768]{0:T(1024)S(1)} %copy-done.38), kind=kOutput, calls=%fused_computation.121 | convolution fusion | flops 17721458688 | bytes 41159680 | tf_op jit(solution)/shard_map/dot_general | solution.py:138
  1915.7 44.5 %psum.14 = f32[2,2048]{1,0:T(2,128)S(1)} all-reduce(f32[2,2048]{1,0:T(2,128)S(1)} %pad_maximum_fusion.6), channel_id=1, replica_groups=mesh['fsdp'=8,'ulysses'=4] {'fsdp','ulysses'}, use_global_device_ids=true, to_apply=%region_13.14 | all-reduce | flops 4096 | bytes 32768 | tf_op jit(solution)/shard_map/psum | solution.py:249
  1960.9 316.9 %all-reduce.3.cloned.1.call-done = bf16[256,22016]{1,0:T(8,128)(2,1)} async-done(((bf16[256,22016]{1,0:T(8,128)(2,1)}), bf16[256,22016]{1,0:T(8,128)(2,1)}) %all-reduce.3.cloned.1.call-update) | async-done | bytes 11272208 | tf_op jit(solution)/shard_map/psum | solution.py:274
  (283 shorter events, 481.2 us)
Async XLA Ops:
  7.2 33.4 %all-gather.11.cloned.1.call-start = ((), (), s32[]{:S(2)}) async-start(), calls=%async_computation.9 | async-start | bytes 2359296 | tf_op jit(solution)/shard_map/all_gather | solution.py:66
  7.9 62.5 %all-gather.13.cloned.1.call-start = ((), (), s32[]{:S(2)}) async-start(), calls=%async_computation.10 | async-start | bytes 2359296 | tf_op jit(solution)/shard_map/all_gather | solution.py:65
  8.7 118.0 %all-gather.15.cloned.1.call-start = ((), (), s32[]{:S(2)}) async-start(), calls=%async_computation.11 | async-start | bytes 9437184 | tf_op jit(solution)/shard_map/all_gather | solution.py:64
  9.4 378.3 %all-gather.17.cloned.1.call-start = ((), (), s32[]{:S(2)}) async-start(), calls=%async_computation.12 | async-start | bytes 9437184 | tf_op jit(solution)/shard_map/all_gather | solution.py:67
  10.0 391.6 %all-gather.21.cloned.1.call-start = ((), (), s32[]{:S(2)}) async-start(), calls=%async_computation.14 | async-start | bytes 25952256 | tf_op jit(solution)/shard_map/all_gather | solution.py:130
  10.6 417.0 %all-gather.23.cloned.1.call-start = ((), (), s32[]{:S(2)}) async-start(), calls=%async_computation.15 | async-start | bytes 25952256 | tf_op jit(solution)/shard_map/all_gather | solution.py:140
  11.1 531.1 %all-gather.19.cloned.1.call-start = ((), (), s32[]{:S(2)}) async-start(), calls=%async_computation.13 | async-start | bytes 25952256 | tf_op jit(solution)/shard_map/all_gather | solution.py:129
  11.9 746.9 %all-gather.25.cloned.1.call-start = ((), (), s32[]{:S(2)}) async-start(), calls=%async_computation.16 | async-start | bytes 51904512 | tf_op jit(solution)/shard_map/all_gather | solution.py:157
  28.3 115.3 %copy-start.26 = (f32[8,1,256]{2,1,0:T(1,128)}, f32[8,1,256]{2,1,0:T(1,128)S(1)}, u32[]{:S(2)}) copy-start(f32[8,1,256]{2,1,0:T(1,128)S(1)} %convert_element_type.245) | copy-start | bytes 24580
  29.0 114.6 %copy-start.33 = (f32[3,256]{1,0:T(4,128)}, f32[3,256]{1,0:T(4,128)S(1)}, u32[]{:S(2)}) copy-start(f32[3,256]{1,0:T(4,128)S(1)} %add_rsqrt_fusion.1) | copy-start | bytes 9220
  48.8 90.2 %all-to-all-start = ((bf16[3,256,4,128]{3,1,0,2:T(8,128)(2,1)}), bf16[3,256,4,128]{3,1,0,2:T(8,128)(2,1)}, u32[]{:S(2)}, u32[]{:S(2)}) async-start(bf16[3,256,4,128]{3,1,0,2:T(8,128)(2,1)} %copy.157), calls=%async_computation | async-start | bytes 1572864 | tf_op jit(solution)/shard_map/all_to_all | solution.py:92
  55.5 98.4 %copy-start.12 = (f32[3,256,128]{1,2,0:T(8,128)}, f32[3,256,128]{1,2,0:T(8,128)S(1)}, u32[]{:S(2)}) copy-start(f32[3,256,128]{1,2,0:T(8,128)S(1)} %get-tuple-element.318) | copy-start | bytes 1179652
  139.1 25.2 %all-to-all-start.1 = ((bf16[3,256,4,128]{1,3,0,2:T(8,128)(2,1)}), bf16[3,256,4,128]{1,3,0,2:T(8,128)(2,1)}, u32[]{:S(2)}, u32[]{:S(2)}) async-start(bf16[3,256,4,128]{1,3,0,2:T(8,128)(2,1)} %copy.160), calls=%async_computation.1 | async-start | bytes 1572864 | tf_op jit(solution)/shard_map/all_to_all | solution.py:91
  164.3 75.1 %all-to-all-start.2 = ((bf16[3,256,16,128]{1,3,0,2:T(8,128)(2,1)}), bf16[3,256,16,128]{1,3,0,2:T(8,128)(2,1)}, u32[]{:S(2)}, u32[]{:S(2)}) async-start(bf16[3,256,16,128]{1,3,0,2:T(8,128)(2,1)} %copy.163), calls=%async_computation.2 | async-start | bytes 6291456 | tf_op jit(solution)/shard_map/all_to_all | solution.py:90
  301.6 75.0 %all-to-all-start.3 = ((bf16[3,1024,4,128]{3,2,0,1:T(4,128)(2,1)}), bf16[3,1024,4,128]{3,2,0,1:T(4,128)(2,1)}, u32[]{:S(2)}, u32[]{:S(2)}) async-start(bf16[3,1024,4,128]{3,2,0,1:T(4,128)(2,1)} %get-tuple-element.103), calls=%async_computation.3 | async-start | bytes 6291456 | tf_op jit(solution)/shard_map/all_to_all | solution.py:122
  306.5 81.2 %copy-start.35 = (f32[768]{0:T(1024)}, f32[768]{0:T(1024)S(1)}, u32[]{:S(2)}) copy-start(f32[768]{0:T(1024)S(1)} %mul.276) | copy-start | bytes 9220
  315.4 82.9 %copy-start.28 = (f32[8,1,256]{2,1,0:T(1,128)}, f32[8,1,256]{2,1,0:T(1,128)S(1)}, u32[]{:S(2)}) copy-start(f32[8,1,256]{2,1,0:T(1,128)S(1)} %convert_element_type.246) | copy-start | bytes 24580
  401.5 140.7 %copy-start.22 = (bf16[768,2048]{1,0:T(8,128)(2,1)}, bf16[768,2048]{1,0:T(8,128)(2,1)S(1)}, u32[]{:S(2)}) copy-start(bf16[768,2048]{1,0:T(8,128)(2,1)S(1)} %multiply_convert_fusion.5) | copy-start | bytes 9437188
  758.8 25.2 %copy-start.8 = (f32[768,2048]{1,0:T(8,128)S(1)}, f32[768,2048]{1,0:T(8,128)}, u32[]{:S(2)}) copy-start(f32[768,2048]{1,0:T(8,128)} %copy-done.7) | copy-start | bytes 18874372
  758.8 25.2 %copy-start.29 = (f32[8,1,256]{2,1,0:T(1,128)S(1)}, f32[8,1,256]{2,1,0:T(1,128)}, u32[]{:S(2)}) copy-start(f32[8,1,256]{2,1,0:T(1,128)} %copy-done.28) | copy-start | bytes 24580
  758.8 25.2 %copy-start.31 = (f32[768]{0:T(1024)S(1)}, f32[768]{0:T(1024)}, u32[]{:S(2)}) copy-start(f32[768]{0:T(1024)} %copy-done.30) | copy-start | bytes 9220
  830.6 75.7 %all-to-all-start.4 = ((bf16[3,256,16,128]{3,1,0,2:T(8,128)(2,1)}), bf16[3,256,16,128]{3,1,0,2:T(8,128)(2,1)S(1)}, u32[]{:S(2)}, u32[]{:S(2)}) async-start(bf16[3,256,16,128]{3,1,0,2:T(8,128)(2,1)} %copy.169), calls=%async_computation.4 | async-start | bytes 6291456 | tf_op jit(solution)/shard_map/all_to_all | solution.py:174
  912.5 185.3 %copy-start.34 = (f32[3,256]{1,0:T(4,128)S(1)}, f32[3,256]{1,0:T(4,128)}, u32[]{:S(2)}) copy-start(f32[3,256]{1,0:T(4,128)} %copy-done.33) | copy-start | bytes 9220
  1094.4 28.8 %all-to-all-start.7 = ((bf16[3,1024,1,128]{3,0,2,1:T(4,128)(2,1)}), bf16[3,1024,1,128]{3,0,2,1:T(4,128)(2,1)S(1)}, u32[]{:S(2)}, u32[]{:S(2)}) async-start(bf16[3,1024,1,128]{3,0,2,1:T(4,128)(2,1)} %copy.184), calls=%async_computation.7 | async-start | bytes 2097152 | tf_op jit(solution)/shard_map/all_to_all | solution.py:213
  1123.2 48.5 %copy-start.19 = (bf16[3,1024,1,128]{3,0,2,1:T(4,128)(2,1)}, bf16[3,1024,1,128]{3,0,2,1:T(4,128)(2,1)S(1)}, u32[]{:S(2)}) copy-start(bf16[3,1024,1,128]{3,0,2,1:T(4,128)(2,1)S(1)} %all-to-all-done.7) | copy-start | bytes 2359300
  1123.2 48.5 %all-to-all-start.6 = ((bf16[3,1024,1,128]{3,0,2,1:T(4,128)(2,1)}), bf16[3,1024,1,128]{3,0,2,1:T(4,128)(2,1)S(1)}, u32[]{:S(2)}, u32[]{:S(2)}) async-start(bf16[3,1024,1,128]{3,0,2,1:T(4,128)(2,1)} %copy.178), calls=%async_computation.6 | async-start | bytes 2097152 | tf_op jit(solution)/shard_map/all_to_all | solution.py:212
  1172.6 82.8 %all-to-all-start.5 = ((bf16[3,1024,4,128]{3,2,0,1:T(4,128)(2,1)}), bf16[3,1024,4,128]{3,2,0,1:T(4,128)(2,1)S(1)}, u32[]{:S(2)}, u32[]{:S(2)}) async-start(bf16[3,1024,4,128]{3,2,0,1:T(4,128)(2,1)} %get-tuple-element.105), calls=%async_computation.5 | async-start | bytes 6291456 | tf_op jit(solution)/shard_map/all_to_all | solution.py:211
  1177.6 712.9 %reduce-scatter.4.cloned.1.call-start = ((), (), s32[]{:S(2)}) async-start(), calls=%async_computation.18 | async-start | bytes 101449728
  1177.6 26.4 %copy-start.37 = (f32[768]{0:T(1024)S(1)}, f32[768]{0:T(1024)}, u32[]{:S(2)}) copy-start(f32[768]{0:T(1024)} %copy-done.35) | copy-start | bytes 9220
  1399.8 490.8 %copy-start.38 = (f32[768]{0:T(1024)S(1)}, f32[768]{0:T(1024)}, u32[]{:S(2)}) copy-start(f32[768]{0:T(1024)} %copy-done.35) | copy-start | bytes 9220
  1399.8 878.0 %all-reduce.3.cloned.1.call-start = ((), (), s32[]{:S(2)}) async-start(), calls=%async_computation.17 | async-start | bytes 22544384 | tf_op jit(solution)/shard_map/psum | solution.py:274
  1890.6 25.1 %copy-start.39 = (f32[2048]{0:T(1024)S(1)}, f32[2048]{0:T(1024)}, u32[]{:S(2)}) copy-start(f32[2048]{0:T(1024)} %get-tuple-element.248) | copy-start | bytes 24580
  (40 other events, 328.3 us)
Sparse Core Ops, SparseCore 0:
  9.9 30.6 all-gather.10
  42.4 27.8 all-gather.12
  72.3 54.3 all-gather.14
  128.4 54.3 all-gather.16
  184.6 116.4 all-gather.20
  302.8 120.9 all-gather.22
  425.7 116.4 all-gather.18
  544.7 214.1 all-gather.24
  1399.9 490.6 reduce-scatter.3
  1892.9 384.8 all-reduce.2
where the time goes:
time: 2330 us; the launch traced here: 2320 us
  waiting for transfers between devices  1370 us (59%)
  matrix products  471 us (20%)
  other arithmetic  181 us (8%)
  local copies, waits for them, and re-layouts  178 us (8%)
  blocking collectives  63.7 us (3%)
  starting transfers between devices  35.7 us (2%)
    unnamed x11, waiting for transfers between devices  495 us
    psum x1, waiting for transfers between devices, on_device(): lax.psum(owner_sums.astype(jnp.bfloat16), 'ulysses').astype(jnp.float32)  317 us
    all_gather x1, waiting for transfers between devices, on_device(): shard_piece = lax.all_gather(stacked_in, 'fsdp', axis=1, tiled=True)  176 us
    all_gather x1, waiting for transfers between devices, on_device(): gate_piece = lax.all_gather(w_gate, 'fsdp', axis=0, tiled=True)  88.7 us
    all_to_all x1, waiting for transfers between devices, on_device(): lax.all_to_all(grad_attended, 'ulysses', split_axis=2, concat_axis=1, til...  71.1 us
    all_to_all x1, waiting for transfers between devices, on_device(): lax.all_to_all(query_sent, 'ulysses', split_axis=2, concat_axis=1, tiled=...  66.7 us
    concatenate x1, other arithmetic, on_device(): jnp.concatenate([jnp.einsum('rc,re->ce', normed_one, grad_attn_mid, prefe...  59.2 us
    all_to_all x1, waiting for transfers between devices, on_device(): lax.all_to_all(attn_heads, 'ulysses', split_axis=1, concat_axis=2, tiled=...  57 us
  transfers between devices with their start and end apart: 18, of which 12 were waited for; matrix products, arithmetic and copies ran while one was open for 17% of the time, Pallas kernels for 0%

commit v1 on v0

--- a/solution.py
+++ b/solution.py
@@ -8,6 +8,22 @@
 KVH = 4
 HD = 128
 epsilon = 1e-05
+
+
+def exchange_in_pairs(value, axis, split, join):
+    ways, here = (lax.axis_size(axis), lax.axis_index(axis))
+    width = value.shape[split] // ways
+    dims = list(value.shape)
+    dims[split] = width
+    height = dims[join]
+    dims[join] = height * ways
+    full = jnp.zeros(dims, value.dtype)
+    for mask in range(ways):
+        part = lax.dynamic_slice_in_dim(value, (here ^ mask) * width, width, axis=split)
+        if mask:
+            part = lax.ppermute(part, axis, [(d, d ^ mask) for d in range(ways)])
+        full = lax.dynamic_update_slice_in_dim(full, part, (here ^ mask) * height, axis=join)
+    return full
 
 
 def rotary_tables(token_positions, head_size):
@@ -171,7 +187,7 @@
         "rd,cd->rc", grad_branch, out_full, preferred_element_type=jnp.float32
     )
     grad_attended = grad_attended.astype(jnp.bfloat16).reshape(seq_count, local_len, H, HD)
-    grad_heads = lax.all_to_all(grad_attended, "ulysses", split_axis=2, concat_axis=1, tiled=True)
+    grad_heads = exchange_in_pairs(grad_attended, "ulysses", 2, 1)
 
     def attend_back(record):
         query_seq, key_seq, value_seq, block_row, log_total, grad_seq = record

time: 2330 us -> 2320 us (level)
    all_to_all x1 -> x0, waiting for transfers between devices: 71.1 us -> none  [on_device(): lax.all_to_all(grad_attended, 'ulysses', split_axis=2, concat_axis=1, til...]
    ppermute x0 -> x3, waiting for transfers between devices: none -> 48.3 us  [exchange_in_pairs(): part = lax.ppermute(part, axis, [(d, d ^ mask) for d in range(ways)])]
  transfers between devices with their start and end apart: 18 -> 20, of which waited for: 12 -> 13; matrix products, arithmetic and copies ran while one was open for 17% -> 17% of each run, Pallas kernels for 0% -> 0%
where the time goes in v1:
time: 2320 us; the launch traced here: 2310 us
  waiting for transfers between devices  1350 us (58%)
  matrix products  471 us (20%)
  local copies, waits for them, and re-layouts  183 us (8%)
  other arithmetic  181 us (8%)
  blocking collectives  63.8 us (3%)
  starting transfers between devices  49.4 us (2%)
    unnamed x11, waiting for transfers between devices  495 us
    psum x1, waiting for transfers between devices, on_device(): lax.psum(owner_sums.astype(jnp.bfloat16), 'ulysses').astype(jnp.float32)  317 us
    all_gather x1, waiting for transfers between devices, on_device(): shard_piece = lax.all_gather(stacked_in, 'fsdp', axis=1, tiled=True)  176 us
    all_gather x1, waiting for transfers between devices, on_device(): gate_piece = lax.all_gather(w_gate, 'fsdp', axis=0, tiled=True)  88.6 us
    all_to_all x1, waiting for transfers between devices, on_device(): lax.all_to_all(query_sent, 'ulysses', split_axis=2, concat_axis=1, tiled=...  66.7 us
    concatenate x1, other arithmetic, on_device(): jnp.concatenate([jnp.einsum('rc,re->ce', normed_one, grad_attn_mid, prefe...  59.2 us
    all_to_all x1, waiting for transfers between devices, on_device(): lax.all_to_all(attn_heads, 'ulysses', split_axis=1, concat_axis=2, tiled=...  56.9 us
    ppermute x3, waiting for transfers between devices, exchange_in_pairs(): part = lax.ppermute(part, axis, [(d, d ^ mask) for d in range(ways)])  48.3 us
  transfers between devices with their start and end apart: 20, of which 13 were waited for; matrix products, arithmetic and copies ran while one was open for 17% of the time, Pallas kernels for 0%

profile of v1, /device:TPU:0, one launch (start us, length us, event | category | flops | bytes accessed | tf_op | source)
XLA Modules:
  0.0 2311.3 jit_solution(4789500883832082768)
XLA Ops:
  55.5 14.9 all-gather.13.cloned.1.call-done
  79.3 47.4 %all-gather.15.cloned.1.call-done = bf16[2048,2048]{1,0:T(8,128)(2,1)} async-done(((bf16[256,2048]{1,0:T(8,128)(2,1)}), bf16[2048,2048]{1,0:T(8,128)(2,1)}) %all-gather.15.cloned.1.call-update) | async-done | bytes 8388624 | tf_op jit(solution)/shard_map/all_gather | solution.py:80
  126.7 12.4 copy.176
  172.7 66.7 %all-to-all-done.2 = bf16[3,256,16,128]{1,3,0,2:T(8,128)(2,1)} async-done(((bf16[3,256,16,128]{1,3,0,2:T(8,128)(2,1)}), bf16[3,256,16,128]{1,3,0,2:T(8,128)(2,1)}, u32[]{:S(2)}, u32[]{:S(2)}) %all-to-all-start.2) | async-done | bytes 3145760 | tf_op jit(solution)/shard_map/all_to_all | solution.py:106
  246.5 55.1 %while.26 = (s32[]{:T(128)}, bf16[3,1024,4,128]{3,2,0,1:T(4,128)(2,1)}, f32[3,1,4,1024]{3,2,1,0:T(4,128)}, bf16[3,1024,1,128]{3,1,0,2:T(8,128)(2,1)}, s32[3,1024...) while((s32[]{:T(128)}, ...), condition=%wide.region_4.5_spmd, body=%wide.region_1.4_spmd.sunk | while | flops 2199384064 | bytes 61486188 | solution.py:137
  319.7 56.9 %all-to-all-done.3 = bf16[3,1024,4,128]{3,2,0,1:T(4,128)(2,1)} async-done(((bf16[3,1024,4,128]{3,2,0,1:T(4,128)(2,1)}), bf16[3,1024,4,128]{3,2,0,1:T(4,128)(2,1)}, u32[]{:S(2)}, u32[]{:S(2)}) %all-to-all-start.3) | async-done | bytes 3145760 | tf_op jit(solution)/shard_map/all_to_all | solution.py:138
  401.5 26.1 %fusion.115 = f32[768,5632]{1,0:T(8,128)} fusion(bf16[768,2048]{1,0:T(8,128)(2,1)S(1)} %multiply_convert_fusion.5, bf16[2048,5632]{1,0:T(8,128)(2,1)} %all-gather.21.cloned.1.call-done), kind=kOutput, calls=%fused_computation.182 | convolution fusion | flops 17716740096 | bytes 43515904 | tf_op jit(solution)/shard_map/dot_general | solution.py:150
  427.6 25.9 %fusion.116 = f32[768,5632]{1,0:T(8,128)} fusion(bf16[768,2048]{1,0:T(8,128)(2,1)} %fusion.73, bf16[5632,2048]{1,0:T(8,128)(2,1)} %all-gather.23.cloned.1.call-done), kind=kOutput, calls=%fused_computation.183 | convolution fusion | flops 17716740096 | bytes 43515904 | tf_op jit(solution)/shard_map/rc,fc->rf/dot_general | solution.py:162
  453.6 88.6 %all-gather.19.cloned.1.call-done = bf16[2048,5632]{1,0:T(8,128)(2,1)} async-done(((bf16[256,5632]{1,0:T(8,128)(2,1)}), bf16[2048,5632]{1,0:T(8,128)(2,1)}) %all-gather.19.cloned.1.call-update) | async-done | bytes 23068688 | tf_op jit(solution)/shard_map/all_gather | solution.py:145
  542.2 40.7 %multiply_convert_fusion.2 = (bf16[768,5632]{1,0:T(8,128)(2,1)}, bf16[768,5632]{1,0:T(8,128)(2,1)}, bf16[768,5632]{1,0:T(8,128)(2,1)}) fusion(f32[768,5632]{1,0:T(8,128)} %fusion.116, f32[768,5632]{1,0:T(8,128)} %fusion.115, bf16[768,2048]{1,0:T(8,128)(2,1)S(1)} %multiply_convert_fusion.5, bf16[2048,5632]{1,0:T(8,128)(2,1)} %all-gather.19.cloned.1.call-done), kind=kOutput, calls=%fused_computation.82 | convolution fusion | flops 17781620736 | bytes 86769664 | tf_op jit(solution)/shard_map/dot_general | solution.py:149
  582.9 176.0 %all-gather.25.cloned.1.call-done = bf16[2,2048,5632]{2,1,0:T(8,128)(2,1)} async-done(((bf16[2,256,5632]{2,1,0:T(8,128)(2,1)}), bf16[2,2048,5632]{2,1,0:T(8,128)(2,1)}) %all-gather.25.cloned.1.call-update) | async-done | bytes 46137360 | tf_op jit(solution)/shard_map/all_gather | solution.py:173
  758.8 25.1 %fusion.67 = f32[768,2048]{1,0:T(8,128)} fusion(bf16[768,5632]{1,0:T(8,128)(2,1)} %get-tuple-element.291, bf16[2,2048,5632]{2,1,0:T(8,128)(2,1)} %all-gather.25.cloned.1.call-done), kind=kOutput, calls=%fused_computation.74 | convolution fusion | flops 17716740096 | bytes 38010880 | tf_op jit(solution)/shard_map/rf,cf->rc/dot_general | solution.py:177
  784.0 27.0 %multiply_reduce_fusion = (f32[2048]{0:T(1024)}, f32[768]{0:T(1024)S(1)}, f32[768,2048]{1,0:T(8,128)}) fusion(f32[768,2048]{1,0:T(8,128)S(1)} %copy-done.8, f32[768]{0:T(1024)S(1)} %copy-done.30, f32[2048]{0:T(1024)S(1)} %bitcast.432, f32[768,2048]{1,0:T(8,128)} %fusion.67, bf16[768,5632]{1,0:T(8,128)(2,1)} %get-tuple-element.290, ...), kind=kOutput, calls=%fused_computation.117 | convolution fusion | flops 17727748096 | bytes 50616320 | tf_op jit(solution)/shard_map/rf,cf->rc/dot_general | solution.py:174
  815.6 11.4 fusion.98
  839.9 27.3 %collective-permute-done = bf16[3,256,4,128]{3,1,2,0:T(8,128)(2,1)} collective-permute-done((bf16[3,256,4,128]{3,1,2,0:T(8,128)(2,1)}, bf16[3,256,4,128]{3,1,2,0:T(8,128)(2,1)}, u32[]{:S(2)}, u32[]{:S(2)}) %collective-permute-start) | collective-permute-done | bytes 786464 | tf_op jit(solution)/shard_map/ppermute | solution.py:24
  868.5 21.0 collective-permute-done.1
  894.4 179.8 %while.27 = (s32[]{:T(128)}, bf16[3,1024,4,128]{3,2,0,1:T(4,128)(2,1)}, bf16[3,1024,1,128]{1,3,2,0:T(8,128)(2,1)}, bf16[3,1024,1,128]{1,3,2,0:T(8,128)(2,1)}, bf...) while((s32[]{:T(128)}, ...), condition=%wide.region_9.10_spmd, body=%wide.region_7.9_spmd.sunk | while | flops 5408944128 | bytes 264601872 | solution.py:223
  916.2 13.6 fusion.185
  975.9 13.6 fusion.185
  1035.7 13.6 fusion.185
  1076.6 17.4 all-to-all-start.6
  1098.8 20.2 all-to-all-done.6
  1122.5 44.8 %convolution_convert_fusion = bf16[2048,11264]{1,0:T(8,128)(2,1)} fusion(bf16[768,2048]{1,0:T(8,128)(2,1)} %copy-done.21, bf16[768,5632]{1,0:T(8,128)(2,1)} %get-tuple-element.291, bf16[768,5632]{1,0:T(8,128)(2,1)} %get-tuple-element.290), kind=kOutput, calls=%fused_computation.72 | convolution fusion | flops 35491151872 | bytes 66584576 | tf_op jit(solution)/shard_map/rc,re->ce/dot_general | solution.py:279
  1173.4 26.2 %convolution_convert_fusion.1 = bf16[2048,5632]{1,0:T(8,128)(2,1)} fusion(bf16[768,2048]{1,0:T(8,128)(2,1)} %fusion.73, bf16[768,5632]{1,0:T(8,128)(2,1)} %get-tuple-element.292), kind=kOutput, calls=%fused_computation.77 | convolution fusion | flops 17728274432 | bytes 34865152 | tf_op jit(solution)/shard_map/rc,re->ce/dot_general | solution.py:282
  1199.6 12.2 convolution_convert_fusion.3
  1211.8 12.3 copy.204
  1323.1 13.2 convolution_convert_fusion.2
  1336.3 59.2 %pad_maximum_fusion = bf16[2048,22016]{1,0:T(8,128)(2,1)} fusion(bf16[2048,5632]{1,0:T(8,128)(2,1)} %convolution_convert_fusion.1, bf16[2048,11264]{1,0:T(8,128)(2,1)} %convolution_convert_fusion, bf16[2048,2048]{1,0:T(8,128)(2,1)} %copy.204, bf16[2048,3072]{1,0:T(8,128)(2,1)} %convolution_convert_fusion.2), kind=kLoop, calls=%fused_computation.71 | loop fusion | flops 360710144 | bytes 180355072 | tf_op jit(solution)/shard_map/concatenate | solution.py:273
  1395.7 490.8 %reduce-scatter.4.cloned.1.call-done = bf16[256,22016]{1,0:T(8,128)(2,1)} async-done(((bf16[2048,22016]{1,0:T(8,128)(2,1)}), bf16[256,22016]{1,0:T(8,128)(2,1)}) %reduce-scatter.4.cloned.1.call-update) | async-done | bytes 11272208
  1886.5 25.1 %add_convert_fusion = bf16[768,2048]{1,0:T(8,128)(2,1)} fusion(f32[768,2048]{1,0:T(8,128)} %copy-done.7, bf16[768,5632]{1,0:T(8,128)(2,1)} %get-tuple-element.292, bf16[5632,2048]{1,0:T(8,128)(2,1)} %all-gather.23.cloned.1.call-done, f32[768]{0:T(1024)S(1)} %copy-done.37), kind=kOutput, calls=%fused_computation.121 | convolution fusion | flops 17721458688 | bytes 41159680 | tf_op jit(solution)/shard_map/dot_general | solution.py:154
  1911.5 44.6 %psum.14 = f32[2,2048]{1,0:T(2,128)S(1)} all-reduce(f32[2,2048]{1,0:T(2,128)S(1)} %pad_maximum_fusion.6), channel_id=1, replica_groups=mesh['fsdp'=8,'ulysses'=4] {'fsdp','ulysses'}, use_global_device_ids=true, to_apply=%region_13.14 | all-reduce | flops 4096 | bytes 32768 | tf_op jit(solution)/shard_map/psum | solution.py:265
  1956.7 316.9 %all-reduce.3.cloned.1.call-done = bf16[256,22016]{1,0:T(8,128)(2,1)} async-done(((bf16[256,22016]{1,0:T(8,128)(2,1)}), bf16[256,22016]{1,0:T(8,128)(2,1)}) %all-reduce.3.cloned.1.call-update) | async-done | bytes 11272208 | tf_op jit(solution)/shard_map/psum | solution.py:290
  (292 shorter events, 504.2 us)
Async XLA Ops:
  7.2 33.4 %all-gather.11.cloned.1.call-start = ((), (), s32[]{:S(2)}) async-start(), calls=%async_computation.8 | async-start | bytes 2359296 | tf_op jit(solution)/shard_map/all_gather | solution.py:82
  7.9 62.5 %all-gather.13.cloned.1.call-start = ((), (), s32[]{:S(2)}) async-start(), calls=%async_computation.9 | async-start | bytes 2359296 | tf_op jit(solution)/shard_map/all_gather | solution.py:81
  8.7 118.0 %all-gather.15.cloned.1.call-start = ((), (), s32[]{:S(2)}) async-start(), calls=%async_computation.10 | async-start | bytes 9437184 | tf_op jit(solution)/shard_map/all_gather | solution.py:80
  9.4 378.3 %all-gather.17.cloned.1.call-start = ((), (), s32[]{:S(2)}) async-start(), calls=%async_computation.11 | async-start | bytes 9437184 | tf_op jit(solution)/shard_map/all_gather | solution.py:83
  10.0 391.6 %all-gather.21.cloned.1.call-start = ((), (), s32[]{:S(2)}) async-start(), calls=%async_computation.13 | async-start | bytes 25952256 | tf_op jit(solution)/shard_map/all_gather | solution.py:146
  10.6 417.1 %all-gather.23.cloned.1.call-start = ((), (), s32[]{:S(2)}) async-start(), calls=%async_computation.14 | async-start | bytes 25952256 | tf_op jit(solution)/shard_map/all_gather | solution.py:156
  11.1 531.1 %all-gather.19.cloned.1.call-start = ((), (), s32[]{:S(2)}) async-start(), calls=%async_computation.12 | async-start | bytes 25952256 | tf_op jit(solution)/shard_map/all_gather | solution.py:145
  11.9 746.9 %all-gather.25.cloned.1.call-start = ((), (), s32[]{:S(2)}) async-start(), calls=%async_computation.15 | async-start | bytes 51904512 | tf_op jit(solution)/shard_map/all_gather | solution.py:173
  28.3 115.4 %copy-start.25 = (f32[8,1,256]{2,1,0:T(1,128)}, f32[8,1,256]{2,1,0:T(1,128)S(1)}, u32[]{:S(2)}) copy-start(f32[8,1,256]{2,1,0:T(1,128)S(1)} %convert_element_type.245) | copy-start | bytes 24580
  29.0 114.6 %copy-start.32 = (f32[3,256]{1,0:T(4,128)}, f32[3,256]{1,0:T(4,128)S(1)}, u32[]{:S(2)}) copy-start(f32[3,256]{1,0:T(4,128)S(1)} %add_rsqrt_fusion.1) | copy-start | bytes 9220
  48.8 90.3 %all-to-all-start = ((bf16[3,256,4,128]{3,1,0,2:T(8,128)(2,1)}), bf16[3,256,4,128]{3,1,0,2:T(8,128)(2,1)}, u32[]{:S(2)}, u32[]{:S(2)}) async-start(bf16[3,256,4,128]{3,1,0,2:T(8,128)(2,1)} %copy.171), calls=%async_computation | async-start | bytes 1572864 | tf_op jit(solution)/shard_map/all_to_all | solution.py:108
  55.5 98.4 %copy-start.11 = (f32[3,256,128]{1,2,0:T(8,128)}, f32[3,256,128]{1,2,0:T(8,128)S(1)}, u32[]{:S(2)}) copy-start(f32[3,256,128]{1,2,0:T(8,128)S(1)} %get-tuple-element.322) | copy-start | bytes 1179652
  139.1 25.2 %all-to-all-start.1 = ((bf16[3,256,4,128]{1,3,0,2:T(8,128)(2,1)}), bf16[3,256,4,128]{1,3,0,2:T(8,128)(2,1)}, u32[]{:S(2)}, u32[]{:S(2)}) async-start(bf16[3,256,4,128]{1,3,0,2:T(8,128)(2,1)} %copy.174), calls=%async_computation.1 | async-start | bytes 1572864 | tf_op jit(solution)/shard_map/all_to_all | solution.py:107
  164.3 75.1 %all-to-all-start.2 = ((bf16[3,256,16,128]{1,3,0,2:T(8,128)(2,1)}), bf16[3,256,16,128]{1,3,0,2:T(8,128)(2,1)}, u32[]{:S(2)}, u32[]{:S(2)}) async-start(bf16[3,256,16,128]{1,3,0,2:T(8,128)(2,1)} %copy.177), calls=%async_computation.2 | async-start | bytes 6291456 | tf_op jit(solution)/shard_map/all_to_all | solution.py:106
  301.6 75.0 %all-to-all-start.3 = ((bf16[3,1024,4,128]{3,2,0,1:T(4,128)(2,1)}), bf16[3,1024,4,128]{3,2,0,1:T(4,128)(2,1)}, u32[]{:S(2)}, u32[]{:S(2)}) async-start(bf16[3,1024,4,128]{3,2,0,1:T(4,128)(2,1)} %get-tuple-element.103), calls=%async_computation.3 | async-start | bytes 6291456 | tf_op jit(solution)/shard_map/all_to_all | solution.py:138
  306.5 81.2 %copy-start.34 = (f32[768]{0:T(1024)}, f32[768]{0:T(1024)S(1)}, u32[]{:S(2)}) copy-start(f32[768]{0:T(1024)S(1)} %mul.300) | copy-start | bytes 9220
  315.4 82.9 %copy-start.27 = (f32[8,1,256]{2,1,0:T(1,128)}, f32[8,1,256]{2,1,0:T(1,128)S(1)}, u32[]{:S(2)}) copy-start(f32[8,1,256]{2,1,0:T(1,128)S(1)} %convert_element_type.246) | copy-start | bytes 24580
  401.5 140.7 %copy-start.21 = (bf16[768,2048]{1,0:T(8,128)(2,1)}, bf16[768,2048]{1,0:T(8,128)(2,1)S(1)}, u32[]{:S(2)}) copy-start(bf16[768,2048]{1,0:T(8,128)(2,1)S(1)} %multiply_convert_fusion.5) | copy-start | bytes 9437188
  758.8 25.1 %copy-start.28 = (f32[8,1,256]{2,1,0:T(1,128)S(1)}, f32[8,1,256]{2,1,0:T(1,128)}, u32[]{:S(2)}) copy-start(f32[8,1,256]{2,1,0:T(1,128)} %copy-done.27) | copy-start | bytes 24580
  758.8 25.1 %copy-start.30 = (f32[768]{0:T(1024)S(1)}, f32[768]{0:T(1024)}, u32[]{:S(2)}) copy-start(f32[768]{0:T(1024)} %copy-done.29) | copy-start | bytes 9220
  831.6 35.7 %collective-permute-start = (bf16[3,256,4,128]{3,1,2,0:T(8,128)(2,1)}, bf16[3,256,4,128]{3,1,2,0:T(8,128)(2,1)}, u32[]{:S(2)}, u32[]{:S(2)}) collective-permute-start(bf16[3,256,4,128]{3,1,2,0:T(8,128)(2,1)} %copy.222), channel_id=1, source_target_pairs={{0,1},{1,0},{2,3},{3,2},{4,5},{5,4},{6,7},{7,6},{8,9},{9,8},{10,11... | collective-permute-start | bytes 2359304 | tf_op jit(solution)/shard_map/ppermute | solution.py:24
  834.1 55.4 %collective-permute-start.1 = (bf16[3,256,4,128]{3,1,2,0:T(8,128)(2,1)}, bf16[3,256,4,128]{3,1,2,0:T(8,128)(2,1)}, u32[]{:S(2)}, u32[]{:S(2)}) collective-permute-start(bf16[3,256,4,128]{3,1,2,0:T(8,128)(2,1)} %copy.223), channel_id=1, source_target_pairs={{0,2},{1,3},{2,0},{3,1},{4,6},{5,7},{6,4},{7,5},{8,10},{9,11},{10,... | collective-permute-start | bytes 2359304 | tf_op jit(solution)/shard_map/ppermute | solution.py:24
  837.5 53.2 %collective-permute-start.2 = (bf16[3,256,4,128]{3,1,2,0:T(8,128)(2,1)}, bf16[3,256,4,128]{3,1,2,0:T(8,128)(2,1)}, u32[]{:S(2)}, u32[]{:S(2)}) collective-permute-start(bf16[3,256,4,128]{3,1,2,0:T(8,128)(2,1)} %copy.224), channel_id=1, source_target_pairs={{0,3},{1,2},{2,1},{3,0},{4,7},{5,6},{6,5},{7,4},{8,11},{9,10},{10,... | collective-permute-start | bytes 2359304 | tf_op jit(solution)/shard_map/ppermute | solution.py:24
  894.4 199.6 %copy-start.33 = (f32[3,256]{1,0:T(4,128)S(1)}, f32[3,256]{1,0:T(4,128)}, u32[]{:S(2)}) copy-start(f32[3,256]{1,0:T(4,128)} %copy-done.32) | copy-start | bytes 9220
  1076.6 42.4 %all-to-all-start.6 = ((bf16[3,1024,1,128]{3,0,2,1:T(4,128)(2,1)}), bf16[3,1024,1,128]{3,0,2,1:T(4,128)(2,1)S(1)}, u32[]{:S(2)}, u32[]{:S(2)}) async-start(bf16[3,1024,1,128]{3,0,2,1:T(4,128)(2,1)} %copy.201), calls=%async_computation.6 | async-start | bytes 2097152 | tf_op jit(solution)/shard_map/all_to_all | solution.py:229
  1119.0 48.4 %copy-start.18 = (bf16[3,1024,1,128]{3,0,2,1:T(4,128)(2,1)}, bf16[3,1024,1,128]{3,0,2,1:T(4,128)(2,1)S(1)}, u32[]{:S(2)}) copy-start(bf16[3,1024,1,128]{3,0,2,1:T(4,128)(2,1)S(1)} %all-to-all-done.6) | copy-start | bytes 2359300
  1119.0 48.4 %all-to-all-start.5 = ((bf16[3,1024,1,128]{3,0,2,1:T(4,128)(2,1)}), bf16[3,1024,1,128]{3,0,2,1:T(4,128)(2,1)S(1)}, u32[]{:S(2)}, u32[]{:S(2)}) async-start(bf16[3,1024,1,128]{3,0,2,1:T(4,128)(2,1)} %copy.195), calls=%async_computation.5 | async-start | bytes 2097152 | tf_op jit(solution)/shard_map/all_to_all | solution.py:228
  1168.4 82.8 %all-to-all-start.4 = ((bf16[3,1024,4,128]{3,2,0,1:T(4,128)(2,1)}), bf16[3,1024,4,128]{3,2,0,1:T(4,128)(2,1)S(1)}, u32[]{:S(2)}, u32[]{:S(2)}) async-start(bf16[3,1024,4,128]{3,2,0,1:T(4,128)(2,1)} %get-tuple-element.105), calls=%async_computation.4 | async-start | bytes 6291456 | tf_op jit(solution)/shard_map/all_to_all | solution.py:227
  1173.4 713.0 %reduce-scatter.4.cloned.1.call-start = ((), (), s32[]{:S(2)}) async-start(), calls=%async_computation.17 | async-start | bytes 101449728
  1173.4 26.2 %copy-start.36 = (f32[768]{0:T(1024)S(1)}, f32[768]{0:T(1024)}, u32[]{:S(2)}) copy-start(f32[768]{0:T(1024)} %copy-done.34) | copy-start | bytes 9220
  1395.6 490.9 %copy-start.37 = (f32[768]{0:T(1024)S(1)}, f32[768]{0:T(1024)}, u32[]{:S(2)}) copy-start(f32[768]{0:T(1024)} %copy-done.34) | copy-start | bytes 9220
  1395.6 878.0 %all-reduce.3.cloned.1.call-start = ((), (), s32[]{:S(2)}) async-start(), calls=%async_computation.16 | async-start | bytes 22544384 | tf_op jit(solution)/shard_map/psum | solution.py:290
  (41 other events, 377.4 us)
Sparse Core Ops, SparseCore 0:
  9.9 30.6 all-gather.10
  42.4 27.8 all-gather.12
  72.3 54.3 all-gather.14
  128.4 54.3 all-gather.16
  184.6 116.4 all-gather.20
  302.8 120.9 all-gather.22
  425.7 116.4 all-gather.18
  544.7 214.1 all-gather.24
  1395.7 490.6 reduce-scatter.3
  1888.8 384.8 all-reduce.2
